TPU v7x, 256 devices: a whole 4x4x8 slice. The times are simulated.
256 devices in a mesh: blk: 32 (over z, x), span: 8 (over y, core).
Axes of the slice: x: 4, y: 4, z: 8, core: 2. Of those that a mesh axis runs over, the one named last changes fastest.
Arguments:
- fluid_adjoint_in: float32 [5, 256, 256, 128], P(None, 'blk', 'span'), may hold values from -4 to 4
- fluid_source: float32 [5, 256, 256, 128], P(None, 'blk', 'span'), may hold values from -24 to 24
- velocity: float32 [3, 256, 256, 128], P(None, 'blk', 'span'), may hold values from 0.1 to 1
- diffusion: float32 [5], replicated, may hold values from 0.5 to 2
- jacobian: float32 [5, 5], replicated, may hold values from -0.4 to 0.4
- wall_coefficient: float32 [32, 256, 128], P('blk', 'span'), may hold values from 0.5 to 2
- metal_costate_prior: float32 [512, 256, 128], P('blk', 'span'), may hold values from -4 to 4
- solid_source: float32 [512, 256, 128], P('blk', 'span'), may hold values from -12 to 12
- conductivity: float32 [512, 256, 128], P('blk', 'span'), may hold values from 0.3 to 3
- tile_owner: int32 [8, 1024, 1], P('span', 'blk'), may hold values from 0 to 31; in each aligned block of 32 rows (0 to 31, 32 to 63, ..., all dimensions but the last counted through in order) at most 3 rows name the same one
- tile_target: int32 [8, 1024], P('span', 'blk'), may hold values from 0 to 31
Outputs:
- fluid_adjoint: float32 [5, 256, 256, 128], P(None, 'blk', 'span')
- solid_adjoint: float32 [512, 256, 128], P('blk', 'span')
- residual_norms: float32 [6], replicated
Inputs may be any that keep to these rules, and one draw needn't show every extreme that they name: `tile_owner`: within the 32 wall tiles of one fluid block (the rows of one device), no owner is named more than 3 times, a bound that some block reaches; every owner is named by some tile.
All inputs are finite; a program needn't handle non-finite values.
Results may differ from a plain program's by a relative error of at most 0.004.
Values sent between devices are 32-bit elements; how exact they have to be, the bound alone decides.
A program may use at most 64 MiB of HBM per device.

v0:
```python
import jax
import jax.numpy as jnp
from jax import lax
from jax.sharding import PartitionSpec as P

FSWEEPS = 4
SSWEEPS = 4
damping_weight = 0.8


def padded(block, sides, width):
    for axis, dim in sides:
        count = lax.axis_size(axis)
        forward = [(i, i + 1) for i in range(count - 1)]
        backward = [(target, source) for source, target in forward]
        low = lax.ppermute(
            lax.slice_in_dim(block, block.shape[dim] - width, None, axis=dim), axis, forward
        )
        high = lax.ppermute(lax.slice_in_dim(block, 0, width, axis=dim), axis, backward)
        block = jnp.concatenate([low, block, high], axis=dim)
    return block


def fluid_operator(bordered_grid_data, velocity, spread, jacobian):
    centre = bordered_grid_data[:, 1:-1, 1:-1, 1:-1]
    x_next = bordered_grid_data[:, 2:, 1:-1, 1:-1]
    y_next = bordered_grid_data[:, 1:-1, 2:, 1:-1]
    z_next = bordered_grid_data[:, 1:-1, 1:-1, 2:]
    beside_all = (
        x_next
        + bordered_grid_data[:, :-2, 1:-1, 1:-1]
        + y_next
        + bordered_grid_data[:, 1:-1, :-2, 1:-1]
        + z_next
        + bordered_grid_data[:, 1:-1, 1:-1, :-2]
    )
    mixing = jnp.einsum("fg,gxyz->fxyz", jacobian, centre, precision=lax.Precision.HIGHEST)
    velocity_sum = velocity[0] + velocity[1] + velocity[2]
    return (
        (6.0 * spread + velocity_sum) * centre
        - spread * beside_all
        - velocity[0] * x_next
        - velocity[1] * y_next
        - velocity[2] * z_next
        + mixing
    )


def face_conductance(kappa_rim):
    centre = kappa_rim[1:-1, 1:-1, 1:-1]
    return (
        0.5 * (centre + kappa_rim[2:, 1:-1, 1:-1]),
        0.5 * (centre + kappa_rim[:-2, 1:-1, 1:-1]),
        0.5 * (centre + kappa_rim[1:-1, 2:, 1:-1]),
        0.5 * (centre + kappa_rim[1:-1, :-2, 1:-1]),
        0.5 * (centre + kappa_rim[1:-1, 1:-1, 2:]),
        0.5 * (centre + kappa_rim[1:-1, 1:-1, :-2]),
    )


def solid_operator(bordered_grid_data, faces, diagonal):
    centre = bordered_grid_data[1:-1, 1:-1, 1:-1]
    flows = (
        faces[0] * bordered_grid_data[2:, 1:-1, 1:-1]
        + faces[1] * bordered_grid_data[:-2, 1:-1, 1:-1]
    )
    flows = (
        flows
        + faces[2] * bordered_grid_data[1:-1, 2:, 1:-1]
        + faces[3] * bordered_grid_data[1:-1, :-2, 1:-1]
    )
    flows = (
        flows
        + faces[4] * bordered_grid_data[1:-1, 1:-1, 2:]
        + faces[5] * bordered_grid_data[1:-1, 1:-1, :-2]
    )
    return diagonal * centre - flows


def pad_depth(array):
    widths = [(0, 0)] * (array.ndim - 1) + [(1, 1)]
    return jnp.pad(array, widths)


def shards(
    fluid_adjoint_in,
    fluid_source,
    velocity,
    diffusion,
    jacobian,
    wall_coefficient,
    metal_costate_prior,
    solid_source,
    conductivity,
    tile_owner,
    tile_target,
):
    highest = lax.Precision.HIGHEST
    spread = diffusion[:, None, None, None]
    fluid_diagonal = (
        6.0 * spread
        + (velocity[0] + velocity[1] + velocity[2])
        + jnp.diagonal(jacobian)[:, None, None, None]
    )
    adjoint = fluid_adjoint_in
    for iteration in range(FSWEEPS):
        bordered_grid_data = padded(adjoint, (("blk", 1), ("span", 2)), 1)
        bordered_grid_data = pad_depth(bordered_grid_data)
        fluid_residual = fluid_source - fluid_operator(
            bordered_grid_data, velocity, spread, jacobian
        )
        adjoint = adjoint + damping_weight * fluid_residual / fluid_diagonal
    fluid_squares = jnp.sum(fluid_residual * fluid_residual, axis=(1, 2, 3))
    wall_flux = wall_coefficient[0] * adjoint[4, 0]
    rows = wall_flux.shape[0]
    blocks = lax.axis_size("blk")
    myself = lax.axis_index("blk")
    owner_local = tile_owner[0, :, 0]
    target_local = tile_target[0, :]
    owners_all, targets_all = (
        lax.all_gather(owner_local, "blk", axis=0, tiled=True),
        lax.all_gather(target_local, "blk", axis=0, tiled=True),
    )
    owner_grid = owners_all.reshape(blocks, rows)
    target_grid = targets_all.reshape(blocks, rows)
    to_myself = owner_grid == myself
    target_hot = target_grid[:, :, None] == jnp.arange(rows, dtype=jnp.int32)[None, None, :]
    placing = (target_hot & to_myself[:, :, None]).astype(jnp.float32).reshape(blocks * rows, rows)
    arrived = lax.all_gather(wall_flux, "blk", axis=0, tiled=True)
    surface = jnp.dot(placing.T, arrived, precision=highest)
    heat_source = solid_source.at[-1].add(surface)
    thermal_state_grid = metal_costate_prior
    kappa_rim = padded(conductivity, (("blk", 0), ("span", 1)), 1)
    kappa_rim = pad_depth(kappa_rim)
    faces = face_conductance(kappa_rim)
    metal_pivot_entries = faces[0] + faces[1] + faces[2] + faces[3] + faces[4] + faces[5]
    for iteration in range(SSWEEPS):
        bordered_grid_data = padded(thermal_state_grid, (("blk", 0), ("span", 1)), 1)
        bordered_grid_data = pad_depth(bordered_grid_data)
        metal_imbalance_grid = heat_source - solid_operator(
            bordered_grid_data, faces, metal_pivot_entries
        )
        thermal_state_grid = (
            thermal_state_grid + damping_weight * metal_imbalance_grid / metal_pivot_entries
        )
    interface_heat_level = thermal_state_grid[-1]
    boundary_patches_finished = lax.all_gather(interface_heat_level, "blk", axis=0, tiled=True)
    output_entries = jnp.take(boundary_patches_finished, owner_local * rows + target_local, axis=0)
    gas_outcome = adjoint.at[4, 0].add(wall_coefficient[0] * output_entries)
    solid_squares = jnp.sum(metal_imbalance_grid * metal_imbalance_grid)[None]
    totals = lax.psum(jnp.concatenate([fluid_squares, solid_squares]), ("blk", "span"))
    every_processor = lax.axis_size("blk") * lax.axis_size("span")
    fluid_cells = float(adjoint.shape[1] * adjoint.shape[2] * adjoint.shape[3] * every_processor)
    solid_cells = float(
        thermal_state_grid.shape[0]
        * thermal_state_grid.shape[1]
        * thermal_state_grid.shape[2]
        * every_processor
    )
    counts = jnp.array([fluid_cells] * 5 + [solid_cells], jnp.float32)
    magnitude_list = jnp.sqrt(totals / counts)
    return (gas_outcome, thermal_state_grid, magnitude_list)


def solution(mesh):
    placed = (
        P(None, "blk", "span", None),
        P(None, "blk", "span", None),
        P(None, "blk", "span", None),
        P(),
        P(),
        P("blk", "span", None),
        P("blk", "span", None),
        P("blk", "span", None),
        P("blk", "span", None),
        P("span", "blk", None),
        P("span", "blk"),
    )
    return jax.shard_map(
        shards,
        mesh=mesh,
        in_specs=placed,
        out_specs=(P(None, "blk", "span", None), P("blk", "span", None), P()),
        check_vma=False,
    )
```

profile of v0, /device:TPU:2, one launch (start us, length us, event | category | flops | bytes accessed | tf_op | source)
XLA Modules:
  0.0 370.5 jit_solution(5415000750408817278)
XLA Ops:
  0.7 1.6 copy.36
  3.0 3.4 collective-permute-start.1
  6.4 2.4 collective-permute-start
  9.6 3.4 collective-permute-start.17
  13.0 2.4 collective-permute-start.16
  15.5 3.4 collective-permute-start.21
  20.5 26.2 %all-reduce.11 = (s32[1024]{0:T(1024)S(1)}, s32[1024]{0:T(1024)S(1)}) all-reduce(s32[1024]{0:T(1024)S(1)} %bitcast_dynamic-update-slice_fusion.1, s32[1024]{0:T(1024)S(1)} %bitcast_dynamic-update-slice_fusion), channel_id=2, replica_groups=mesh['blk'=32,'span'=8] {'blk'}, use_global_device_ids=true, to_apply=%add.9 | all-reduce | flops 2048 | bytes 16384
  47.4 2.5 collective-permute-start.20
  50.5 1.3 collective-permute-start.2
  51.8 3.0 collective-permute-start.3
  56.2 3.7 %collective-permute-start.19 = (f32[18,1,128]{2,1,0:T(1,128)S(1)}, f32[18,1,128]{2,1,0:T(1,128)S(1)}, u32[]{:S(2)}, u32[]{:S(2)}) collective-permute-start(f32[18,1,128]{2,1,0:T(1,128)S(1)} %get-tuple-element.70), channel_id=1, source_target_pairs={{0,1},{1,2},{2,3},{3,4},{4,5},{5,6},{6,7},{8,9},{9,10},{10,11},{11... | collective-permute-start | bytes 27656 | tf_op jit(solution)/shard_map/ppermute | solution.py:16
  60.7 2.7 fusion.10
  63.4 1.9 collective-permute-start.4
  65.4 3.9 %collective-permute-start.5 = (f32[5,1,32,128]{3,0,2,1:T(8,128)S(1)}, f32[5,1,32,128]{3,0,2,1:T(8,128)S(1)}, u32[]{:S(2)}, u32[]{:S(2)}) collective-permute-start(f32[5,1,32,128]{3,0,2,1:T(8,128)S(1)} %get-tuple-element.56), channel_id=1, source_target_pairs={{0,8},{8,16},{16,24},{24,32},{32,40},{40,48},{48,56},{56,64},{64,7... | collective-permute-start | bytes 245768 | tf_op jit(solution)/shard_map/ppermute | solution.py:16
  69.3 1.7 collective-permute-done.4
  71.0 1.9 collective-permute-done.5
  72.9 1.3 collective-permute-start.6
  74.2 3.1 collective-permute-start.7
  79.0 2.2 fusion.11
  81.2 1.9 collective-permute-start.8
  83.1 4.2 %collective-permute-start.9 = (f32[5,1,32,128]{3,0,2,1:T(8,128)S(1)}, f32[5,1,32,128]{3,0,2,1:T(8,128)S(1)}, u32[]{:S(2)}, u32[]{:S(2)}) collective-permute-start(f32[5,1,32,128]{3,0,2,1:T(8,128)S(1)} %get-tuple-element.54), channel_id=1, source_target_pairs={{0,8},{8,16},{16,24},{24,32},{32,40},{40,48},{48,56},{56,64},{64,7... | collective-permute-start | bytes 245768 | tf_op jit(solution)/shard_map/ppermute | solution.py:16
  87.3 1.4 collective-permute-done.8
  88.7 1.8 collective-permute-done.9
  91.8 3.3 collective-permute-start.11
  96.5 5.7 %collective-permute-start.23 = (f32[18,1,128]{2,1,0:T(1,128)S(1)}, f32[18,1,128]{2,1,0:T(1,128)S(1)}, u32[]{:S(2)}, u32[]{:S(2)}) collective-permute-start(f32[18,1,128]{2,1,0:T(1,128)S(1)} %get-tuple-element.72), channel_id=1, source_target_pairs={{0,1},{1,2},{2,3},{3,4},{4,5},{5,6},{6,7},{8,9},{9,10},{10,11},{11... | collective-permute-start | bytes 27656 | tf_op jit(solution)/shard_map/ppermute | solution.py:16
  103.0 2.2 fusion.12
  105.2 1.9 collective-permute-start.12
  107.2 3.9 %collective-permute-start.13 = (f32[5,1,32,128]{3,0,2,1:T(8,128)S(1)}, f32[5,1,32,128]{3,0,2,1:T(8,128)S(1)}, u32[]{:S(2)}, u32[]{:S(2)}) collective-permute-start(f32[5,1,32,128]{3,0,2,1:T(8,128)S(1)} %get-tuple-element.52), channel_id=1, source_target_pairs={{0,8},{8,16},{16,24},{24,32},{32,40},{40,48},{48,56},{56,64},{64,7... | collective-permute-start | bytes 245768 | tf_op jit(solution)/shard_map/ppermute | solution.py:16
  112.4 2.3 collective-permute-done.13
  114.7 1.4 collective-permute-start.14
  116.2 3.1 collective-permute-start.15
  121.0 2.5 multiply_reduce_fusion
  123.5 59.1 %all_gather.14 = f32[1024,128]{1,0:T(8,128)S(1)} all-gather(f32[32,128]{1,0:T(8,128)S(1)} %bitcast_multiply_fusion), channel_id=1, replica_groups=mesh['blk'=32,'span'=8] {'blk'}, dimensions={0}, use_global_device_ids=true | all-gather | bytes 540672 | tf_op jit(solution)/shard_map/all_gather | solution.py:129
  184.0 1.9 collective-permute-start.24
  186.0 3.9 %collective-permute-start.25 = (f32[1,32,128]{2,1,0:T(8,128)S(1)}, f32[1,32,128]{2,1,0:T(8,128)S(1)}, u32[]{:S(2)}, u32[]{:S(2)}) collective-permute-start(f32[1,32,128]{2,1,0:T(8,128)S(1)} %get-tuple-element.78), channel_id=1, source_target_pairs={{0,8},{8,16},{16,24},{24,32},{32,40},{40,48},{48,56},{56,64},{64,7... | collective-permute-start | bytes 49160 | tf_op jit(solution)/shard_map/ppermute | solution.py:16
  189.9 1.7 collective-permute-done.25
  191.6 1.3 collective-permute-start.26
  192.9 3.0 collective-permute-start.27
  197.5 1.9 collective-permute-start.28
  199.4 3.9 %collective-permute-start.29 = (f32[1,32,128]{2,1,0:T(8,128)S(1)}, f32[1,32,128]{2,1,0:T(8,128)S(1)}, u32[]{:S(2)}, u32[]{:S(2)}) collective-permute-start(f32[1,32,128]{2,1,0:T(8,128)S(1)} %get-tuple-element.76), channel_id=1, source_target_pairs={{0,8},{8,16},{16,24},{24,32},{32,40},{40,48},{48,56},{56,64},{64,7... | collective-permute-start | bytes 49160 | tf_op jit(solution)/shard_map/ppermute | solution.py:16
  203.4 1.7 collective-permute-done.29
  206.4 5.1 %collective-permute-start.31 = (f32[18,1,128]{2,1,0:T(1,128)S(1)}, f32[18,1,128]{2,1,0:T(1,128)S(1)}, u32[]{:S(2)}, u32[]{:S(2)}) collective-permute-start(f32[18,1,128]{2,1,0:T(1,128)S(1)} %get-tuple-element.66), channel_id=1, source_target_pairs={{0,1},{1,2},{2,3},{3,4},{4,5},{5,6},{6,7},{8,9},{9,10},{10,11},{11... | collective-permute-start | bytes 27656 | tf_op jit(solution)/shard_map/ppermute | solution.py:16
  213.1 1.9 collective-permute-start.32
  215.0 4.2 %collective-permute-start.33 = (f32[1,32,128]{2,1,0:T(8,128)S(1)}, f32[1,32,128]{2,1,0:T(8,128)S(1)}, u32[]{:S(2)}, u32[]{:S(2)}) collective-permute-start(f32[1,32,128]{2,1,0:T(8,128)S(1)} %get-tuple-element.74), channel_id=1, source_target_pairs={{0,8},{8,16},{16,24},{24,32},{32,40},{40,48},{48,56},{56,64},{64,7... | collective-permute-start | bytes 49160 | tf_op jit(solution)/shard_map/ppermute | solution.py:16
  219.3 1.4 collective-permute-done.33
  222.0 4.8 %collective-permute-start.35 = (f32[18,1,128]{2,1,0:T(1,128)S(1)}, f32[18,1,128]{2,1,0:T(1,128)S(1)}, u32[]{:S(2)}, u32[]{:S(2)}) collective-permute-start(f32[18,1,128]{2,1,0:T(1,128)S(1)} %get-tuple-element.64), channel_id=1, source_target_pairs={{0,1},{1,2},{2,3},{3,4},{4,5},{5,6},{6,7},{8,9},{9,10},{10,11},{11... | collective-permute-start | bytes 27656 | tf_op jit(solution)/shard_map/ppermute | solution.py:16
  229.6 89.1 %psum.7 = f32[6]{0:T(128)S(1)} all-reduce(f32[6]{0:T(128)S(1)} %pad_maximum_fusion.78), channel_id=1, replica_groups=mesh['blk'=32,'span'=8] {'blk','span'}, use_global_device_ids=true, to_apply=%region_2.3 | all-reduce | flops 6 | bytes 48 | tf_op jit(solution)/shard_map/psum | solution.py:151
  318.9 49.3 %all-gather.2 = f32[1,1024,128]{2,1,0:T(8,128)S(1)} all-gather(f32[1,32,128]{2,1,0:T(8,128)S(1)} %slice.616), channel_id=4, replica_groups=mesh['blk'=32,'span'=8] {'blk'}, dimensions={1}, use_global_device_ids=true | all-gather | bytes 540672 | tf_op jit(solution)/shard_map/all_gather | solution.py:147
  (137 shorter events, 26.1 us)
Async XLA Ops:
  0.6 46.1 %copy-start = (f32[5,5]{1,0:T(8,128)S(1)}, f32[5,5]{1,0:T(8,128)}, u32[]{:S(2)}) copy-start(f32[5,5]{1,0:T(8,128)} %param.20) | copy-start | bytes 304
  0.6 18.4 %copy-start.18 = (u32[256]{0:T(256)S(1)}, u32[256]{0:T(256)}, u32[]{:S(2)}) copy-start(u32[256]{0:T(256)} %constant.146) | copy-start | bytes 3076
  0.7 49.3 %copy-start.3 = (f32[5,8,32,128]{3,2,1,0:T(8,128)S(1)}, f32[5,8,32,128]{3,2,1,0:T(8,128)}, u32[]{:S(2)}) copy-start(f32[5,8,32,128]{3,2,1,0:T(8,128)} %param.16) | copy-start | bytes 1966084
  0.7 49.2 %copy-start.1 = (f32[16,32,128]{2,1,0:T(8,128)S(1)}, f32[16,32,128]{2,1,0:T(8,128)}, u32[]{:S(2)}) copy-start(f32[16,32,128]{2,1,0:T(8,128)} %param.24) | copy-start | bytes 786436
  0.7 19.6 %copy-start.17 = (s32[1,32,1]{1,2,0:T(1,128)S(1)}, s32[1,32,1]{1,2,0:T(1,128)}, u32[]{:S(2)}) copy-start(s32[1,32,1]{1,2,0:T(1,128)} %param.25) | copy-start | bytes 388
  0.7 19.7 %copy-start.16 = (s32[1,32]{1,0:T(1,128)S(1)}, s32[1,32]{1,0:T(1,128)}, u32[]{:S(2)}) copy-start(s32[1,32]{1,0:T(1,128)} %param.26) | copy-start | bytes 388
  3.0 46.9 %collective-permute-start.1 = (f32[5,1,32,128]{3,0,2,1:T(8,128)}, f32[5,1,32,128]{3,0,2,1:T(8,128)S(1)}, u32[]{:S(2)}, u32[]{:S(2)}) collective-permute-start(f32[5,1,32,128]{3,0,2,1:T(8,128)} %get-tuple-element.59), channel_id=1, source_target_pairs={{0,8},{8,16},{16,24},{24,32},{32,40},{40,48},{48,56},{56,64},{64,7... | collective-permute-start | bytes 245768 | tf_op jit(solution)/shard_map/ppermute | solution.py:16
  6.4 44.0 %collective-permute-start = (f32[5,1,32,128]{3,0,2,1:T(8,128)}, f32[5,1,32,128]{3,0,2,1:T(8,128)S(1)}, u32[]{:S(2)}, u32[]{:S(2)}) collective-permute-start(f32[5,1,32,128]{3,0,2,1:T(8,128)} %get-tuple-element.58), channel_id=1, source_target_pairs={{8,0},{16,8},{24,16},{32,24},{40,32},{48,40},{56,48},{64,56},{72,6... | collective-permute-start | bytes 245768 | tf_op jit(solution)/shard_map/ppermute | solution.py:19
  9.6 37.7 %collective-permute-start.17 = (f32[1,32,128]{2,1,0:T(8,128)S(1)}, f32[1,32,128]{2,1,0:T(8,128)S(1)}, u32[]{:S(2)}, u32[]{:S(2)}) collective-permute-start(f32[1,32,128]{2,1,0:T(8,128)S(1)} %get-tuple-element.80), channel_id=1, source_target_pairs={{0,8},{8,16},{16,24},{24,32},{32,40},{40,48},{48,56},{56,64},{64,7... | collective-permute-start | bytes 49160 | tf_op jit(solution)/shard_map/ppermute | solution.py:16
  13.0 36.9 %collective-permute-start.16 = (f32[1,32,128]{2,1,0:T(8,128)S(1)}, f32[1,32,128]{2,1,0:T(8,128)S(1)}, u32[]{:S(2)}, u32[]{:S(2)}) collective-permute-start(f32[1,32,128]{2,1,0:T(8,128)S(1)} %get-tuple-element.81), channel_id=1, source_target_pairs={{8,0},{16,8},{24,16},{32,24},{40,32},{48,40},{56,48},{64,56},{72,6... | collective-permute-start | bytes 49160 | tf_op jit(solution)/shard_map/ppermute | solution.py:19
  15.5 49.9 %collective-permute-start.21 = (f32[1,32,128]{2,1,0:T(8,128)S(1)}, f32[1,32,128]{2,1,0:T(8,128)S(1)}, u32[]{:S(2)}, u32[]{:S(2)}) collective-permute-start(f32[1,32,128]{2,1,0:T(8,128)S(1)} %get-tuple-element.83), channel_id=1, source_target_pairs={{0,8},{8,16},{16,24},{24,32},{32,40},{40,48},{48,56},{56,64},{64,7... | collective-permute-start | bytes 49160 | tf_op jit(solution)/shard_map/ppermute | solution.py:16
  19.0 84.0 %copy-start.7 = (f32[8,32,128]{2,1,0:T(8,128)}, f32[8,32,128]{2,1,0:T(8,128)S(1)}, u32[]{:S(2)}) copy-start(f32[8,32,128]{2,1,0:T(8,128)S(1)} %get-tuple-element.61) | copy-start | bytes 393220
  19.0 84.0 %copy-start.9 = (f32[8,32,128]{2,1,0:T(8,128)}, f32[8,32,128]{2,1,0:T(8,128)S(1)}, u32[]{:S(2)}) copy-start(f32[8,32,128]{2,1,0:T(8,128)S(1)} %get-tuple-element.62) | copy-start | bytes 393220
  19.0 84.0 %copy-start.11 = (f32[8,32,128]{2,1,0:T(8,128)}, f32[8,32,128]{2,1,0:T(8,128)S(1)}, u32[]{:S(2)}) copy-start(f32[8,32,128]{2,1,0:T(8,128)S(1)} %get-tuple-element.63) | copy-start | bytes 393220
  47.4 39.9 %collective-permute-start.20 = (f32[1,32,128]{2,1,0:T(8,128)S(1)}, f32[1,32,128]{2,1,0:T(8,128)S(1)}, u32[]{:S(2)}, u32[]{:S(2)}) collective-permute-start(f32[1,32,128]{2,1,0:T(8,128)S(1)} %get-tuple-element.82), channel_id=1, source_target_pairs={{8,0},{16,8},{24,16},{32,24},{40,32},{48,40},{56,48},{64,56},{72,6... | collective-permute-start | bytes 49160 | tf_op jit(solution)/shard_map/ppermute | solution.py:19
  50.5 5.7 %collective-permute-start.2 = (f32[5,10,1,128]{3,0,2,1:T(8,128)S(1)}, f32[5,10,1,128]{3,0,2,1:T(8,128)S(1)}, u32[]{:S(2)}, u32[]{:S(2)}) collective-permute-start(f32[5,10,1,128]{3,0,2,1:T(8,128)S(1)} %get-tuple-element.49), channel_id=1, source_target_pairs={{1,0},{2,1},{3,2},{4,3},{5,4},{6,5},{7,6},{9,8},{10,9},{11,10},{12... | collective-permute-start | bytes 76808 | tf_op jit(solution)/shard_map/ppermute | solution.py:19
  51.8 8.1 %collective-permute-start.3 = (f32[5,10,1,128]{3,0,2,1:T(8,128)S(1)}, f32[5,10,1,128]{3,0,2,1:T(8,128)S(1)}, u32[]{:S(2)}, u32[]{:S(2)}) collective-permute-start(f32[5,10,1,128]{3,0,2,1:T(8,128)S(1)} %get-tuple-element.48), channel_id=1, source_target_pairs={{0,1},{1,2},{2,3},{3,4},{4,5},{5,6},{6,7},{8,9},{9,10},{10,11},{11... | collective-permute-start | bytes 76808 | tf_op jit(solution)/shard_map/ppermute | solution.py:16
  54.8 52.3 %collective-permute-start.18 = (f32[18,1,128]{2,1,0:T(1,128)S(1)}, f32[18,1,128]{2,1,0:T(1,128)S(1)}, u32[]{:S(2)}, u32[]{:S(2)}) collective-permute-start(f32[18,1,128]{2,1,0:T(1,128)S(1)} %get-tuple-element.71), channel_id=1, source_target_pairs={{1,0},{2,1},{3,2},{4,3},{5,4},{6,5},{7,6},{9,8},{10,9},{11,10},{12... | collective-permute-start | bytes 27656 | tf_op jit(solution)/shard_map/ppermute | solution.py:19
  56.2 54.9 %collective-permute-start.19 = (f32[18,1,128]{2,1,0:T(1,128)S(1)}, f32[18,1,128]{2,1,0:T(1,128)S(1)}, u32[]{:S(2)}, u32[]{:S(2)}) collective-permute-start(f32[18,1,128]{2,1,0:T(1,128)S(1)} %get-tuple-element.70), channel_id=1, source_target_pairs={{0,1},{1,2},{2,3},{3,4},{4,5},{5,6},{6,7},{8,9},{9,10},{10,11},{11... | collective-permute-start | bytes 27656 | tf_op jit(solution)/shard_map/ppermute | solution.py:16
  63.4 7.5 %collective-permute-start.4 = (f32[5,1,32,128]{3,0,2,1:T(8,128)S(1)}, f32[5,1,32,128]{3,0,2,1:T(8,128)S(1)}, u32[]{:S(2)}, u32[]{:S(2)}) collective-permute-start(f32[5,1,32,128]{3,0,2,1:T(8,128)S(1)} %get-tuple-element.57), channel_id=1, source_target_pairs={{8,0},{16,8},{24,16},{32,24},{40,32},{48,40},{56,48},{64,56},{72,6... | collective-permute-start | bytes 245768 | tf_op jit(solution)/shard_map/ppermute | solution.py:19
  65.4 7.5 %collective-permute-start.5 = (f32[5,1,32,128]{3,0,2,1:T(8,128)S(1)}, f32[5,1,32,128]{3,0,2,1:T(8,128)S(1)}, u32[]{:S(2)}, u32[]{:S(2)}) collective-permute-start(f32[5,1,32,128]{3,0,2,1:T(8,128)S(1)} %get-tuple-element.56), channel_id=1, source_target_pairs={{0,8},{8,16},{16,24},{24,32},{32,40},{40,48},{48,56},{56,64},{64,7... | collective-permute-start | bytes 245768 | tf_op jit(solution)/shard_map/ppermute | solution.py:16
  72.9 4.4 %collective-permute-start.6 = (f32[5,10,1,128]{3,0,2,1:T(8,128)S(1)}, f32[5,10,1,128]{3,0,2,1:T(8,128)S(1)}, u32[]{:S(2)}, u32[]{:S(2)}) collective-permute-start(f32[5,10,1,128]{3,0,2,1:T(8,128)S(1)} %get-tuple-element.47), channel_id=1, source_target_pairs={{1,0},{2,1},{3,2},{4,3},{5,4},{6,5},{7,6},{9,8},{10,9},{11,10},{12... | collective-permute-start | bytes 76808 | tf_op jit(solution)/shard_map/ppermute | solution.py:19
  74.2 3.9 %collective-permute-start.7 = (f32[5,10,1,128]{3,0,2,1:T(8,128)S(1)}, f32[5,10,1,128]{3,0,2,1:T(8,128)S(1)}, u32[]{:S(2)}, u32[]{:S(2)}) collective-permute-start(f32[5,10,1,128]{3,0,2,1:T(8,128)S(1)} %get-tuple-element.46), channel_id=1, source_target_pairs={{0,1},{1,2},{2,3},{3,4},{4,5},{5,6},{6,7},{8,9},{9,10},{10,11},{11... | collective-permute-start | bytes 76808 | tf_op jit(solution)/shard_map/ppermute | solution.py:16
  81.2 7.5 %collective-permute-start.8 = (f32[5,1,32,128]{3,0,2,1:T(8,128)S(1)}, f32[5,1,32,128]{3,0,2,1:T(8,128)S(1)}, u32[]{:S(2)}, u32[]{:S(2)}) collective-permute-start(f32[5,1,32,128]{3,0,2,1:T(8,128)S(1)} %get-tuple-element.55), channel_id=1, source_target_pairs={{8,0},{16,8},{24,16},{32,24},{40,32},{48,40},{56,48},{64,56},{72,6... | collective-permute-start | bytes 245768 | tf_op jit(solution)/shard_map/ppermute | solution.py:19
  83.1 7.4 %collective-permute-start.9 = (f32[5,1,32,128]{3,0,2,1:T(8,128)S(1)}, f32[5,1,32,128]{3,0,2,1:T(8,128)S(1)}, u32[]{:S(2)}, u32[]{:S(2)}) collective-permute-start(f32[5,1,32,128]{3,0,2,1:T(8,128)S(1)} %get-tuple-element.54), channel_id=1, source_target_pairs={{0,8},{8,16},{16,24},{24,32},{32,40},{40,48},{48,56},{56,64},{64,7... | collective-permute-start | bytes 245768 | tf_op jit(solution)/shard_map/ppermute | solution.py:16
  90.5 6.0 %collective-permute-start.10 = (f32[5,10,1,128]{3,0,2,1:T(8,128)S(1)}, f32[5,10,1,128]{3,0,2,1:T(8,128)S(1)}, u32[]{:S(2)}, u32[]{:S(2)}) collective-permute-start(f32[5,10,1,128]{3,0,2,1:T(8,128)S(1)} %get-tuple-element.45), channel_id=1, source_target_pairs={{1,0},{2,1},{3,2},{4,3},{5,4},{6,5},{7,6},{9,8},{10,9},{11,10},{12... | collective-permute-start | bytes 76808 | tf_op jit(solution)/shard_map/ppermute | solution.py:19
  91.8 10.4 %collective-permute-start.11 = (f32[5,10,1,128]{3,0,2,1:T(8,128)S(1)}, f32[5,10,1,128]{3,0,2,1:T(8,128)S(1)}, u32[]{:S(2)}, u32[]{:S(2)}) collective-permute-start(f32[5,10,1,128]{3,0,2,1:T(8,128)S(1)} %get-tuple-element.44), channel_id=1, source_target_pairs={{0,1},{1,2},{2,3},{3,4},{4,5},{5,6},{6,7},{8,9},{9,10},{10,11},{11... | collective-permute-start | bytes 76808 | tf_op jit(solution)/shard_map/ppermute | solution.py:16
  95.2 24.1 %collective-permute-start.22 = (f32[18,1,128]{2,1,0:T(1,128)S(1)}, f32[18,1,128]{2,1,0:T(1,128)S(1)}, u32[]{:S(2)}, u32[]{:S(2)}) collective-permute-start(f32[18,1,128]{2,1,0:T(1,128)S(1)} %get-tuple-element.73), channel_id=1, source_target_pairs={{1,0},{2,1},{3,2},{4,3},{5,4},{6,5},{7,6},{9,8},{10,9},{11,10},{12... | collective-permute-start | bytes 27656 | tf_op jit(solution)/shard_map/ppermute | solution.py:19
  96.5 22.8 %collective-permute-start.23 = (f32[18,1,128]{2,1,0:T(1,128)S(1)}, f32[18,1,128]{2,1,0:T(1,128)S(1)}, u32[]{:S(2)}, u32[]{:S(2)}) collective-permute-start(f32[18,1,128]{2,1,0:T(1,128)S(1)} %get-tuple-element.72), channel_id=1, source_target_pairs={{0,1},{1,2},{2,3},{3,4},{4,5},{5,6},{6,7},{8,9},{9,10},{10,11},{11... | collective-permute-start | bytes 27656 | tf_op jit(solution)/shard_map/ppermute | solution.py:16
  105.2 7.2 %collective-permute-start.12 = (f32[5,1,32,128]{3,0,2,1:T(8,128)S(1)}, f32[5,1,32,128]{3,0,2,1:T(8,128)S(1)}, u32[]{:S(2)}, u32[]{:S(2)}) collective-permute-start(f32[5,1,32,128]{3,0,2,1:T(8,128)S(1)} %get-tuple-element.53), channel_id=1, source_target_pairs={{8,0},{16,8},{24,16},{32,24},{40,32},{48,40},{56,48},{64,56},{72,6... | collective-permute-start | bytes 245768 | tf_op jit(solution)/shard_map/ppermute | solution.py:19
  107.2 7.5 %collective-permute-start.13 = (f32[5,1,32,128]{3,0,2,1:T(8,128)S(1)}, f32[5,1,32,128]{3,0,2,1:T(8,128)S(1)}, u32[]{:S(2)}, u32[]{:S(2)}) collective-permute-start(f32[5,1,32,128]{3,0,2,1:T(8,128)S(1)} %get-tuple-element.52), channel_id=1, source_target_pairs={{0,8},{8,16},{16,24},{24,32},{32,40},{40,48},{48,56},{56,64},{64,7... | collective-permute-start | bytes 245768 | tf_op jit(solution)/shard_map/ppermute | solution.py:16
  114.7 4.9 %collective-permute-start.14 = (f32[5,10,1,128]{3,0,2,1:T(8,128)S(1)}, f32[5,10,1,128]{3,0,2,1:T(8,128)S(1)}, u32[]{:S(2)}, u32[]{:S(2)}) collective-permute-start(f32[5,10,1,128]{3,0,2,1:T(8,128)S(1)} %get-tuple-element.43), channel_id=1, source_target_pairs={{1,0},{2,1},{3,2},{4,3},{5,4},{6,5},{7,6},{9,8},{10,9},{11,10},{12... | collective-permute-start | bytes 76808 | tf_op jit(solution)/shard_map/ppermute | solution.py:19
  116.2 3.9 %collective-permute-start.15 = (f32[5,10,1,128]{3,0,2,1:T(8,128)S(1)}, f32[5,10,1,128]{3,0,2,1:T(8,128)S(1)}, u32[]{:S(2)}, u32[]{:S(2)}) collective-permute-start(f32[5,10,1,128]{3,0,2,1:T(8,128)S(1)} %get-tuple-element.42), channel_id=1, source_target_pairs={{0,1},{1,2},{2,3},{3,4},{4,5},{5,6},{6,7},{8,9},{9,10},{10,11},{11... | collective-permute-start | bytes 76808 | tf_op jit(solution)/shard_map/ppermute | solution.py:16
  121.0 61.6 %copy-start.2 = (f32[16,32,128]{2,1,0:T(8,128)S(1)}, f32[16,32,128]{2,1,0:T(8,128)}, u32[]{:S(2)}) copy-start(f32[16,32,128]{2,1,0:T(8,128)} %param.23) | copy-start | bytes 786436
  184.0 5.9 %collective-permute-start.24 = (f32[1,32,128]{2,1,0:T(8,128)S(1)}, f32[1,32,128]{2,1,0:T(8,128)S(1)}, u32[]{:S(2)}, u32[]{:S(2)}) collective-permute-start(f32[1,32,128]{2,1,0:T(8,128)S(1)} %get-tuple-element.79), channel_id=1, source_target_pairs={{8,0},{16,8},{24,16},{32,24},{40,32},{48,40},{56,48},{64,56},{72,6... | collective-permute-start | bytes 49160 | tf_op jit(solution)/shard_map/ppermute | solution.py:19
  186.0 5.6 %collective-permute-start.25 = (f32[1,32,128]{2,1,0:T(8,128)S(1)}, f32[1,32,128]{2,1,0:T(8,128)S(1)}, u32[]{:S(2)}, u32[]{:S(2)}) collective-permute-start(f32[1,32,128]{2,1,0:T(8,128)S(1)} %get-tuple-element.78), channel_id=1, source_target_pairs={{0,8},{8,16},{16,24},{24,32},{32,40},{40,48},{48,56},{56,64},{64,7... | collective-permute-start | bytes 49160 | tf_op jit(solution)/shard_map/ppermute | solution.py:16
  191.6 4.3 %collective-permute-start.26 = (f32[18,1,128]{2,1,0:T(1,128)S(1)}, f32[18,1,128]{2,1,0:T(1,128)S(1)}, u32[]{:S(2)}, u32[]{:S(2)}) collective-permute-start(f32[18,1,128]{2,1,0:T(1,128)S(1)} %get-tuple-element.69), channel_id=1, source_target_pairs={{1,0},{2,1},{3,2},{4,3},{5,4},{6,5},{7,6},{9,8},{10,9},{11,10},{12... | collective-permute-start | bytes 27656 | tf_op jit(solution)/shard_map/ppermute | solution.py:19
  192.9 3.9 %collective-permute-start.27 = (f32[18,1,128]{2,1,0:T(1,128)S(1)}, f32[18,1,128]{2,1,0:T(1,128)S(1)}, u32[]{:S(2)}, u32[]{:S(2)}) collective-permute-start(f32[18,1,128]{2,1,0:T(1,128)S(1)} %get-tuple-element.68), channel_id=1, source_target_pairs={{0,1},{1,2},{2,3},{3,4},{4,5},{5,6},{6,7},{8,9},{9,10},{10,11},{11... | collective-permute-start | bytes 27656 | tf_op jit(solution)/shard_map/ppermute | solution.py:16
  197.5 5.9 %collective-permute-start.28 = (f32[1,32,128]{2,1,0:T(8,128)S(1)}, f32[1,32,128]{2,1,0:T(8,128)S(1)}, u32[]{:S(2)}, u32[]{:S(2)}) collective-permute-start(f32[1,32,128]{2,1,0:T(8,128)S(1)} %get-tuple-element.77), channel_id=1, source_target_pairs={{8,0},{16,8},{24,16},{32,24},{40,32},{48,40},{56,48},{64,56},{72,6... | collective-permute-start | bytes 49160 | tf_op jit(solution)/shard_map/ppermute | solution.py:19
  199.4 5.6 %collective-permute-start.29 = (f32[1,32,128]{2,1,0:T(8,128)S(1)}, f32[1,32,128]{2,1,0:T(8,128)S(1)}, u32[]{:S(2)}, u32[]{:S(2)}) collective-permute-start(f32[1,32,128]{2,1,0:T(8,128)S(1)} %get-tuple-element.76), channel_id=1, source_target_pairs={{0,8},{8,16},{16,24},{24,32},{32,40},{40,48},{48,56},{56,64},{64,7... | collective-permute-start | bytes 49160 | tf_op jit(solution)/shard_map/ppermute | solution.py:16
  205.1 6.4 %collective-permute-start.30 = (f32[18,1,128]{2,1,0:T(1,128)S(1)}, f32[18,1,128]{2,1,0:T(1,128)S(1)}, u32[]{:S(2)}, u32[]{:S(2)}) collective-permute-start(f32[18,1,128]{2,1,0:T(1,128)S(1)} %get-tuple-element.67), channel_id=1, source_target_pairs={{1,0},{2,1},{3,2},{4,3},{5,4},{6,5},{7,6},{9,8},{10,9},{11,10},{12... | collective-permute-start | bytes 27656 | tf_op jit(solution)/shard_map/ppermute | solution.py:19
  206.4 5.9 %collective-permute-start.31 = (f32[18,1,128]{2,1,0:T(1,128)S(1)}, f32[18,1,128]{2,1,0:T(1,128)S(1)}, u32[]{:S(2)}, u32[]{:S(2)}) collective-permute-start(f32[18,1,128]{2,1,0:T(1,128)S(1)} %get-tuple-element.66), channel_id=1, source_target_pairs={{0,1},{1,2},{2,3},{3,4},{4,5},{5,6},{6,7},{8,9},{9,10},{10,11},{11... | collective-permute-start | bytes 27656 | tf_op jit(solution)/shard_map/ppermute | solution.py:16
  213.1 6.2 %collective-permute-start.32 = (f32[1,32,128]{2,1,0:T(8,128)S(1)}, f32[1,32,128]{2,1,0:T(8,128)S(1)}, u32[]{:S(2)}, u32[]{:S(2)}) collective-permute-start(f32[1,32,128]{2,1,0:T(8,128)S(1)} %get-tuple-element.75), channel_id=1, source_target_pairs={{8,0},{16,8},{24,16},{32,24},{40,32},{48,40},{56,48},{64,56},{72,6... | collective-permute-start | bytes 49160 | tf_op jit(solution)/shard_map/ppermute | solution.py:19
  215.0 5.6 %collective-permute-start.33 = (f32[1,32,128]{2,1,0:T(8,128)S(1)}, f32[1,32,128]{2,1,0:T(8,128)S(1)}, u32[]{:S(2)}, u32[]{:S(2)}) collective-permute-start(f32[1,32,128]{2,1,0:T(8,128)S(1)} %get-tuple-element.74), channel_id=1, source_target_pairs={{0,8},{8,16},{16,24},{24,32},{32,40},{40,48},{48,56},{56,64},{64,7... | collective-permute-start | bytes 49160 | tf_op jit(solution)/shard_map/ppermute | solution.py:16
  220.7 6.1 %collective-permute-start.34 = (f32[18,1,128]{2,1,0:T(1,128)S(1)}, f32[18,1,128]{2,1,0:T(1,128)S(1)}, u32[]{:S(2)}, u32[]{:S(2)}) collective-permute-start(f32[18,1,128]{2,1,0:T(1,128)S(1)} %get-tuple-element.65), channel_id=1, source_target_pairs={{1,0},{2,1},{3,2},{4,3},{5,4},{6,5},{7,6},{9,8},{10,9},{11,10},{12... | collective-permute-start | bytes 27656 | tf_op jit(solution)/shard_map/ppermute | solution.py:19
  222.0 5.6 %collective-permute-start.35 = (f32[18,1,128]{2,1,0:T(1,128)S(1)}, f32[18,1,128]{2,1,0:T(1,128)S(1)}, u32[]{:S(2)}, u32[]{:S(2)}) collective-permute-start(f32[18,1,128]{2,1,0:T(1,128)S(1)} %get-tuple-element.64), channel_id=1, source_target_pairs={{0,1},{1,2},{2,3},{3,4},{4,5},{5,6},{6,7},{8,9},{9,10},{10,11},{11... | collective-permute-start | bytes 27656 | tf_op jit(solution)/shard_map/ppermute | solution.py:16
  228.9 141.1 %copy-start.19 = (f32[6]{0:T(128)S(1)}, f32[6]{0:T(128)}, u32[]{:S(2)}) copy-start(f32[6]{0:T(128)} %constant.130) | copy-start | bytes 76
  318.9 51.6 %copy-start.6 = (f32[16,32,128]{2,1,0:T(8,128)}, f32[16,32,128]{2,1,0:T(8,128)S(1)}, u32[]{:S(2)}) copy-start(f32[16,32,128]{2,1,0:T(8,128)S(1)} %divide_add_fusion) | copy-start | bytes 786436
  (8 other events, 83.2 us)
where the time goes:
time: 372 us; the launch traced here: 370 us
  blocking collectives  224 us (60%)
  starting transfers between devices  99.9 us (27%)
  waiting for transfers between devices  18.5 us (5%)
  matrix products  10.4 us (3%)
  other arithmetic  8.88 us (2%)
  local copies, waits for them, and re-layouts  6.83 us (2%)
    psum x1, blocking collectives, shards(): lax.psum(jnp.concatenate([fluid_squares, solid_squares]), ('blk', 'span'))  89.1 us
    ppermute x18, starting transfers between devices, padded(): lax.ppermute(lax.slice_in_dim(block, block.shape[dim] - width, None, axis...  69.2 us
    all_gather x1, blocking collectives, shards(): arrived = lax.all_gather(wall_flux, 'blk', axis=0, tiled=True)  59.1 us
    all_gather x1, blocking collectives, shards(): lax.all_gather(interface_heat_level, 'blk', axis=0, tiled=True)  49.3 us
    ppermute x18, starting transfers between devices, padded(): lax.ppermute(lax.slice_in_dim(block, 0, width, axis=dim), axis, backward)  30.7 us
    unnamed x1, blocking collectives  26.2 us
    ppermute x18, waiting for transfers between devices, padded(): lax.ppermute(lax.slice_in_dim(block, block.shape[dim] - width, None, axis...  14.4 us
    dot_general x4, matrix products, fluid_operator(): jnp.einsum('fg,gxyz->fxyz', jacobian, centre, precision=lax.Precision.HIG...  9.52 us
  transfers between devices with their start and end apart: 36, of which 14 were waited for; matrix products, arithmetic and copies ran while one was open for 4% of the time, Pallas kernels for 0%

commit v1 on v0

--- a/solution.py
+++ b/solution.py
@@ -6,6 +6,13 @@
 FSWEEPS = 4
 SSWEEPS = 4
 damping_weight = 0.8
+
+
+def gather_over(value, name, d):
+    count = lax.axis_size(name)
+    blocks = jnp.stack([value for _ in range(count)])
+    blocks = lax.all_to_all(blocks, name, split_axis=0, concat_axis=0)
+    return jnp.concatenate(blocks, axis=d)
 
 
 def padded(block, sides, width):
@@ -144,7 +151,7 @@
             thermal_state_grid + damping_weight * metal_imbalance_grid / metal_pivot_entries
         )
     interface_heat_level = thermal_state_grid[-1]
-    boundary_patches_finished = lax.all_gather(interface_heat_level, "blk", axis=0, tiled=True)
+    boundary_patches_finished = gather_over(interface_heat_level, "blk", 0)
     output_entries = jnp.take(boundary_patches_finished, owner_local * rows + target_local, axis=0)
     gas_outcome = adjoint.at[4, 0].add(wall_coefficient[0] * output_entries)
     solid_squares = jnp.sum(metal_imbalance_grid * metal_imbalance_grid)[None]

time: 372 us -> 334 us (0.90)
  blocking collectives: 224 us -> 166 us
  starting transfers between devices: 99.9 us -> 119 us
    all_gather x1 -> x0, blocking collectives: 49.3 us -> none  [shards(): lax.all_gather(interface_heat_level, 'blk', axis=0, tiled=True)]
    all_to_all x0 -> x1, starting transfers between devices: none -> 18.7 us  [gather_over(): blocks = lax.all_to_all(blocks, name, split_axis=0, concat_axis=0)]
    psum x1, blocking collectives: 89.1 us -> 80.8 us  [shards(): lax.psum(jnp.concatenate([fluid_squares, solid_squares]), ('blk', 'span'))]
  transfers between devices with their start and end apart: 36 -> 37, of which waited for: 14 -> 14; matrix products, arithmetic and copies ran while one was open for 4% -> 4% of each run, Pallas kernels for 0% -> 0%
where the time goes in v1:
time: 334 us; the launch traced here: 331 us
  blocking collectives  166 us (50%)
  starting transfers between devices  119 us (36%)
  waiting for transfers between devices  18.3 us (5%)
  matrix products  10 us (3%)
  other arithmetic  8.9 us (3%)
  local copies, waits for them, and re-layouts  6.96 us (2%)
    psum x1, blocking collectives, shards(): lax.psum(jnp.concatenate([fluid_squares, solid_squares]), ('blk', 'span'))  80.8 us
    ppermute x18, starting transfers between devices, padded(): lax.ppermute(lax.slice_in_dim(block, block.shape[dim] - width, None, axis...  69.4 us
    all_gather x1, blocking collectives, shards(): arrived = lax.all_gather(wall_flux, 'blk', axis=0, tiled=True)  59.1 us
    ppermute x18, starting transfers between devices, padded(): lax.ppermute(lax.slice_in_dim(block, 0, width, axis=dim), axis, backward)  30.6 us
    unnamed x1, blocking collectives  26.2 us
    all_to_all x1, starting transfers between devices, gather_over(): blocks = lax.all_to_all(blocks, name, split_axis=0, concat_axis=0)  18.7 us
    ppermute x18, waiting for transfers between devices, padded(): lax.ppermute(lax.slice_in_dim(block, block.shape[dim] - width, None, axis...  14.3 us
    dot_general x4, matrix products, fluid_operator(): jnp.einsum('fg,gxyz->fxyz', jacobian, centre, precision=lax.Precision.HIG...  9.13 us
  transfers between devices with their start and end apart: 37, of which 14 were waited for; matrix products, arithmetic and copies ran while one was open for 4% of the time, Pallas kernels for 0%

profile of v1, /device:TPU:2, one launch (start us, length us, event | category | flops | bytes accessed | tf_op | source)
XLA Modules:
  0.0 331.3 jit_solution(13422069845040126709)
XLA Ops:
  0.7 1.6 copy.36
  2.4 3.4 %collective-permute-start.1 = (f32[5,1,32,128]{3,0,2,1:T(8,128)S(1)}, f32[5,1,32,128]{3,0,2,1:T(8,128)S(1)}, u32[]{:S(2)}, u32[]{:S(2)}) collective-permute-start(f32[5,1,32,128]{3,0,2,1:T(8,128)S(1)} %get-tuple-element.59), channel_id=1, source_target_pairs={{0,8},{8,16},{16,24},{24,32},{32,40},{40,48},{48,56},{56,64},{64,7... | collective-permute-start | bytes 245768 | tf_op jit(solution)/shard_map/ppermute | solution.py:23
  5.8 2.4 collective-permute-start
  9.0 3.4 %collective-permute-start.17 = (f32[1,32,128]{2,1,0:T(8,128)S(1)}, f32[1,32,128]{2,1,0:T(8,128)S(1)}, u32[]{:S(2)}, u32[]{:S(2)}) collective-permute-start(f32[1,32,128]{2,1,0:T(8,128)S(1)} %get-tuple-element.80), channel_id=1, source_target_pairs={{0,8},{8,16},{16,24},{24,32},{32,40},{40,48},{48,56},{56,64},{64,7... | collective-permute-start | bytes 49160 | tf_op jit(solution)/shard_map/ppermute | solution.py:23
  12.3 2.4 collective-permute-start.16
  14.8 3.4 %collective-permute-start.21 = (f32[1,32,128]{2,1,0:T(8,128)S(1)}, f32[1,32,128]{2,1,0:T(8,128)S(1)}, u32[]{:S(2)}, u32[]{:S(2)}) collective-permute-start(f32[1,32,128]{2,1,0:T(8,128)S(1)} %get-tuple-element.83), channel_id=1, source_target_pairs={{0,8},{8,16},{16,24},{24,32},{32,40},{40,48},{48,56},{56,64},{64,7... | collective-permute-start | bytes 49160 | tf_op jit(solution)/shard_map/ppermute | solution.py:23
  19.8 26.2 %all-reduce.11 = (s32[1024]{0:T(1024)S(1)}, s32[1024]{0:T(1024)S(1)}) all-reduce(s32[1024]{0:T(1024)S(1)} %bitcast_dynamic-update-slice_fusion.1, s32[1024]{0:T(1024)S(1)} %bitcast_dynamic-update-slice_fusion), channel_id=2, replica_groups=mesh['blk'=32,'span'=8] {'blk'}, use_global_device_ids=true, to_apply=%add.9 | all-reduce | flops 2048 | bytes 16384
  46.7 2.5 collective-permute-start.20
  49.8 1.3 collective-permute-start.2
  51.1 3.0 collective-permute-start.3
  55.4 3.7 %collective-permute-start.19 = (f32[18,1,128]{2,1,0:T(1,128)S(1)}, f32[18,1,128]{2,1,0:T(1,128)S(1)}, u32[]{:S(2)}, u32[]{:S(2)}) collective-permute-start(f32[18,1,128]{2,1,0:T(1,128)S(1)} %get-tuple-element.70), channel_id=1, source_target_pairs={{0,1},{1,2},{2,3},{3,4},{4,5},{5,6},{6,7},{8,9},{9,10},{10,11},{11... | collective-permute-start | bytes 27656 | tf_op jit(solution)/shard_map/ppermute | solution.py:23
  60.0 2.6 fusion.10
  62.6 1.9 collective-permute-start.4
  64.6 3.9 %collective-permute-start.5 = (f32[5,1,32,128]{3,0,2,1:T(8,128)S(1)}, f32[5,1,32,128]{3,0,2,1:T(8,128)S(1)}, u32[]{:S(2)}, u32[]{:S(2)}) collective-permute-start(f32[5,1,32,128]{3,0,2,1:T(8,128)S(1)} %get-tuple-element.56), channel_id=1, source_target_pairs={{0,8},{8,16},{16,24},{24,32},{32,40},{40,48},{48,56},{56,64},{64,7... | collective-permute-start | bytes 245768 | tf_op jit(solution)/shard_map/ppermute | solution.py:23
  68.5 1.6 collective-permute-done.4
  70.2 1.9 collective-permute-done.5
  72.1 1.3 collective-permute-start.6
  73.4 3.1 collective-permute-start.7
  78.2 2.1 fusion.11
  80.3 1.9 collective-permute-start.8
  82.2 4.2 %collective-permute-start.9 = (f32[5,1,32,128]{3,0,2,1:T(8,128)S(1)}, f32[5,1,32,128]{3,0,2,1:T(8,128)S(1)}, u32[]{:S(2)}, u32[]{:S(2)}) collective-permute-start(f32[5,1,32,128]{3,0,2,1:T(8,128)S(1)} %get-tuple-element.54), channel_id=1, source_target_pairs={{0,8},{8,16},{16,24},{24,32},{32,40},{40,48},{48,56},{56,64},{64,7... | collective-permute-start | bytes 245768 | tf_op jit(solution)/shard_map/ppermute | solution.py:23
  86.4 1.4 collective-permute-done.8
  87.8 1.8 collective-permute-done.9
  90.9 3.4 %collective-permute-start.11 = (f32[5,10,1,128]{3,0,2,1:T(8,128)S(1)}, f32[5,10,1,128]{3,0,2,1:T(8,128)S(1)}, u32[]{:S(2)}, u32[]{:S(2)}) collective-permute-start(f32[5,10,1,128]{3,0,2,1:T(8,128)S(1)} %get-tuple-element.44), channel_id=1, source_target_pairs={{0,1},{1,2},{2,3},{3,4},{4,5},{5,6},{6,7},{8,9},{9,10},{10,11},{11... | collective-permute-start | bytes 76808 | tf_op jit(solution)/shard_map/ppermute | solution.py:23
  94.2 1.3 collective-permute-start.22
  95.5 5.7 %collective-permute-start.23 = (f32[18,1,128]{2,1,0:T(1,128)S(1)}, f32[18,1,128]{2,1,0:T(1,128)S(1)}, u32[]{:S(2)}, u32[]{:S(2)}) collective-permute-start(f32[18,1,128]{2,1,0:T(1,128)S(1)} %get-tuple-element.72), channel_id=1, source_target_pairs={{0,1},{1,2},{2,3},{3,4},{4,5},{5,6},{6,7},{8,9},{9,10},{10,11},{11... | collective-permute-start | bytes 27656 | tf_op jit(solution)/shard_map/ppermute | solution.py:23
  102.1 2.1 fusion.12
  104.2 1.9 collective-permute-start.12
  106.1 3.9 %collective-permute-start.13 = (f32[5,1,32,128]{3,0,2,1:T(8,128)S(1)}, f32[5,1,32,128]{3,0,2,1:T(8,128)S(1)}, u32[]{:S(2)}, u32[]{:S(2)}) collective-permute-start(f32[5,1,32,128]{3,0,2,1:T(8,128)S(1)} %get-tuple-element.52), channel_id=1, source_target_pairs={{0,8},{8,16},{16,24},{24,32},{32,40},{40,48},{48,56},{56,64},{64,7... | collective-permute-start | bytes 245768 | tf_op jit(solution)/shard_map/ppermute | solution.py:23
  111.4 2.3 collective-permute-done.13
  114.9 3.1 collective-permute-start.15
  119.7 2.4 multiply_reduce_fusion
  122.2 59.1 %all_gather.11 = f32[1024,128]{1,0:T(8,128)S(1)} all-gather(f32[32,128]{1,0:T(8,128)S(1)} %bitcast_multiply_fusion), channel_id=1, replica_groups=mesh['blk'=32,'span'=8] {'blk'}, dimensions={0}, use_global_device_ids=true | all-gather | bytes 540672 | tf_op jit(solution)/shard_map/all_gather | solution.py:136
  182.7 1.9 collective-permute-start.24
  184.7 3.9 %collective-permute-start.25 = (f32[1,32,128]{2,1,0:T(8,128)S(1)}, f32[1,32,128]{2,1,0:T(8,128)S(1)}, u32[]{:S(2)}, u32[]{:S(2)}) collective-permute-start(f32[1,32,128]{2,1,0:T(8,128)S(1)} %get-tuple-element.78), channel_id=1, source_target_pairs={{0,8},{8,16},{16,24},{24,32},{32,40},{40,48},{48,56},{56,64},{64,7... | collective-permute-start | bytes 49160 | tf_op jit(solution)/shard_map/ppermute | solution.py:23
  188.6 1.7 collective-permute-done.25
  190.3 1.3 collective-permute-start.26
  191.6 3.0 collective-permute-start.27
  196.2 1.9 collective-permute-start.28
  198.1 3.9 %collective-permute-start.29 = (f32[1,32,128]{2,1,0:T(8,128)S(1)}, f32[1,32,128]{2,1,0:T(8,128)S(1)}, u32[]{:S(2)}, u32[]{:S(2)}) collective-permute-start(f32[1,32,128]{2,1,0:T(8,128)S(1)} %get-tuple-element.76), channel_id=1, source_target_pairs={{0,8},{8,16},{16,24},{24,32},{32,40},{40,48},{48,56},{56,64},{64,7... | collective-permute-start | bytes 49160 | tf_op jit(solution)/shard_map/ppermute | solution.py:23
  202.1 1.7 collective-permute-done.29
  205.1 5.1 %collective-permute-start.31 = (f32[18,1,128]{2,1,0:T(1,128)S(1)}, f32[18,1,128]{2,1,0:T(1,128)S(1)}, u32[]{:S(2)}, u32[]{:S(2)}) collective-permute-start(f32[18,1,128]{2,1,0:T(1,128)S(1)} %get-tuple-element.66), channel_id=1, source_target_pairs={{0,1},{1,2},{2,3},{3,4},{4,5},{5,6},{6,7},{8,9},{9,10},{10,11},{11... | collective-permute-start | bytes 27656 | tf_op jit(solution)/shard_map/ppermute | solution.py:23
  211.8 1.9 collective-permute-start.32
  213.7 4.2 %collective-permute-start.33 = (f32[1,32,128]{2,1,0:T(8,128)S(1)}, f32[1,32,128]{2,1,0:T(8,128)S(1)}, u32[]{:S(2)}, u32[]{:S(2)}) collective-permute-start(f32[1,32,128]{2,1,0:T(8,128)S(1)} %get-tuple-element.74), channel_id=1, source_target_pairs={{0,8},{8,16},{16,24},{24,32},{32,40},{40,48},{48,56},{56,64},{64,7... | collective-permute-start | bytes 49160 | tf_op jit(solution)/shard_map/ppermute | solution.py:23
  217.9 1.4 collective-permute-done.33
  220.7 5.0 %collective-permute-start.35 = (f32[18,1,128]{2,1,0:T(1,128)S(1)}, f32[18,1,128]{2,1,0:T(1,128)S(1)}, u32[]{:S(2)}, u32[]{:S(2)}) collective-permute-start(f32[18,1,128]{2,1,0:T(1,128)S(1)} %get-tuple-element.64), channel_id=1, source_target_pairs={{0,1},{1,2},{2,3},{3,4},{4,5},{5,6},{6,7},{8,9},{9,10},{10,11},{11... | collective-permute-start | bytes 27656 | tf_op jit(solution)/shard_map/ppermute | solution.py:23
  228.7 18.7 %all-to-all-start = ((f32[32,32,128]{2,1,0:T(8,128)}), f32[32,32,128]{2,1,0:T(8,128)S(1)}, u32[]{:S(2)}, u32[]{:S(2)}) async-start(f32[32,32,128]{2,1,0:T(8,128)} %stack.3), calls=%async_computation | async-start | bytes 1048576 | tf_op jit(solution)/shard_map/all_to_all | solution.py:14
  248.2 80.8 %psum.7 = f32[6]{0:T(128)S(1)} all-reduce(f32[6]{0:T(128)S(1)} %pad_maximum_fusion.78), channel_id=1, replica_groups=mesh['blk'=32,'span'=8] {'blk','span'}, use_global_device_ids=true, to_apply=%region_2.3 | all-reduce | flops 6 | bytes 48 | tf_op jit(solution)/shard_map/psum | solution.py:158
  (127 shorter events, 26.1 us)
Async XLA Ops:
  0.6 45.4 %copy-start = (f32[5,5]{1,0:T(8,128)S(1)}, f32[5,5]{1,0:T(8,128)}, u32[]{:S(2)}) copy-start(f32[5,5]{1,0:T(8,128)} %param.20) | copy-start | bytes 304
  0.6 17.7 %copy-start.12 = (u32[256]{0:T(256)S(1)}, u32[256]{0:T(256)}, u32[]{:S(2)}) copy-start(u32[256]{0:T(256)} %constant.146) | copy-start | bytes 3076
  0.7 48.6 %copy-start.3 = (f32[5,8,32,128]{3,2,1,0:T(8,128)S(1)}, f32[5,8,32,128]{3,2,1,0:T(8,128)}, u32[]{:S(2)}) copy-start(f32[5,8,32,128]{3,2,1,0:T(8,128)} %param.16) | copy-start | bytes 1966084
  0.7 17.6 %copy-start.5 = (f32[3,8,32,128]{3,2,1,0:T(8,128)S(1)}, f32[3,8,32,128]{3,2,1,0:T(8,128)}, u32[]{:S(2)}) copy-start(f32[3,8,32,128]{3,2,1,0:T(8,128)} %param.18) | copy-start | bytes 1179652
  0.7 17.6 %copy-start.9 = (f32[5]{0:T(128)S(1)}, f32[5]{0:T(128)}, u32[]{:S(2)}) copy-start(f32[5]{0:T(128)} %param.19) | copy-start | bytes 64
  0.7 48.5 %copy-start.1 = (f32[16,32,128]{2,1,0:T(8,128)S(1)}, f32[16,32,128]{2,1,0:T(8,128)}, u32[]{:S(2)}) copy-start(f32[16,32,128]{2,1,0:T(8,128)} %param.24) | copy-start | bytes 786436
  0.7 18.9 %copy-start.11 = (s32[1,32,1]{1,2,0:T(1,128)S(1)}, s32[1,32,1]{1,2,0:T(1,128)}, u32[]{:S(2)}) copy-start(s32[1,32,1]{1,2,0:T(1,128)} %param.25) | copy-start | bytes 388
  0.7 19.0 %copy-start.10 = (s32[1,32]{1,0:T(1,128)S(1)}, s32[1,32]{1,0:T(1,128)}, u32[]{:S(2)}) copy-start(s32[1,32]{1,0:T(1,128)} %param.26) | copy-start | bytes 388
  2.4 46.9 %collective-permute-start.1 = (f32[5,1,32,128]{3,0,2,1:T(8,128)S(1)}, f32[5,1,32,128]{3,0,2,1:T(8,128)S(1)}, u32[]{:S(2)}, u32[]{:S(2)}) collective-permute-start(f32[5,1,32,128]{3,0,2,1:T(8,128)S(1)} %get-tuple-element.59), channel_id=1, source_target_pairs={{0,8},{8,16},{16,24},{24,32},{32,40},{40,48},{48,56},{56,64},{64,7... | collective-permute-start | bytes 245768 | tf_op jit(solution)/shard_map/ppermute | solution.py:23
  5.8 44.0 %collective-permute-start = (f32[5,1,32,128]{3,0,2,1:T(8,128)S(1)}, f32[5,1,32,128]{3,0,2,1:T(8,128)S(1)}, u32[]{:S(2)}, u32[]{:S(2)}) collective-permute-start(f32[5,1,32,128]{3,0,2,1:T(8,128)S(1)} %get-tuple-element.58), channel_id=1, source_target_pairs={{8,0},{16,8},{24,16},{32,24},{40,32},{48,40},{56,48},{64,56},{72,6... | collective-permute-start | bytes 245768 | tf_op jit(solution)/shard_map/ppermute | solution.py:26
  9.0 37.7 %collective-permute-start.17 = (f32[1,32,128]{2,1,0:T(8,128)S(1)}, f32[1,32,128]{2,1,0:T(8,128)S(1)}, u32[]{:S(2)}, u32[]{:S(2)}) collective-permute-start(f32[1,32,128]{2,1,0:T(8,128)S(1)} %get-tuple-element.80), channel_id=1, source_target_pairs={{0,8},{8,16},{16,24},{24,32},{32,40},{40,48},{48,56},{56,64},{64,7... | collective-permute-start | bytes 49160 | tf_op jit(solution)/shard_map/ppermute | solution.py:23
  12.3 36.9 %collective-permute-start.16 = (f32[1,32,128]{2,1,0:T(8,128)S(1)}, f32[1,32,128]{2,1,0:T(8,128)S(1)}, u32[]{:S(2)}, u32[]{:S(2)}) collective-permute-start(f32[1,32,128]{2,1,0:T(8,128)S(1)} %get-tuple-element.81), channel_id=1, source_target_pairs={{8,0},{16,8},{24,16},{32,24},{40,32},{48,40},{56,48},{64,56},{72,6... | collective-permute-start | bytes 49160 | tf_op jit(solution)/shard_map/ppermute | solution.py:26
  14.8 49.7 %collective-permute-start.21 = (f32[1,32,128]{2,1,0:T(8,128)S(1)}, f32[1,32,128]{2,1,0:T(8,128)S(1)}, u32[]{:S(2)}, u32[]{:S(2)}) collective-permute-start(f32[1,32,128]{2,1,0:T(8,128)S(1)} %get-tuple-element.83), channel_id=1, source_target_pairs={{0,8},{8,16},{16,24},{24,32},{32,40},{40,48},{48,56},{56,64},{64,7... | collective-permute-start | bytes 49160 | tf_op jit(solution)/shard_map/ppermute | solution.py:23
  46.7 39.7 %collective-permute-start.20 = (f32[1,32,128]{2,1,0:T(8,128)S(1)}, f32[1,32,128]{2,1,0:T(8,128)S(1)}, u32[]{:S(2)}, u32[]{:S(2)}) collective-permute-start(f32[1,32,128]{2,1,0:T(8,128)S(1)} %get-tuple-element.82), channel_id=1, source_target_pairs={{8,0},{16,8},{24,16},{32,24},{40,32},{48,40},{56,48},{64,56},{72,6... | collective-permute-start | bytes 49160 | tf_op jit(solution)/shard_map/ppermute | solution.py:26
  49.8 5.7 %collective-permute-start.2 = (f32[5,10,1,128]{3,0,2,1:T(8,128)S(1)}, f32[5,10,1,128]{3,0,2,1:T(8,128)S(1)}, u32[]{:S(2)}, u32[]{:S(2)}) collective-permute-start(f32[5,10,1,128]{3,0,2,1:T(8,128)S(1)} %get-tuple-element.49), channel_id=1, source_target_pairs={{1,0},{2,1},{3,2},{4,3},{5,4},{6,5},{7,6},{9,8},{10,9},{11,10},{12... | collective-permute-start | bytes 76808 | tf_op jit(solution)/shard_map/ppermute | solution.py:26
  51.1 8.1 %collective-permute-start.3 = (f32[5,10,1,128]{3,0,2,1:T(8,128)S(1)}, f32[5,10,1,128]{3,0,2,1:T(8,128)S(1)}, u32[]{:S(2)}, u32[]{:S(2)}) collective-permute-start(f32[5,10,1,128]{3,0,2,1:T(8,128)S(1)} %get-tuple-element.48), channel_id=1, source_target_pairs={{0,1},{1,2},{2,3},{3,4},{4,5},{5,6},{6,7},{8,9},{9,10},{10,11},{11... | collective-permute-start | bytes 76808 | tf_op jit(solution)/shard_map/ppermute | solution.py:23
  54.1 52.0 %collective-permute-start.18 = (f32[18,1,128]{2,1,0:T(1,128)S(1)}, f32[18,1,128]{2,1,0:T(1,128)S(1)}, u32[]{:S(2)}, u32[]{:S(2)}) collective-permute-start(f32[18,1,128]{2,1,0:T(1,128)S(1)} %get-tuple-element.71), channel_id=1, source_target_pairs={{1,0},{2,1},{3,2},{4,3},{5,4},{6,5},{7,6},{9,8},{10,9},{11,10},{12... | collective-permute-start | bytes 27656 | tf_op jit(solution)/shard_map/ppermute | solution.py:26
  55.4 54.6 %collective-permute-start.19 = (f32[18,1,128]{2,1,0:T(1,128)S(1)}, f32[18,1,128]{2,1,0:T(1,128)S(1)}, u32[]{:S(2)}, u32[]{:S(2)}) collective-permute-start(f32[18,1,128]{2,1,0:T(1,128)S(1)} %get-tuple-element.70), channel_id=1, source_target_pairs={{0,1},{1,2},{2,3},{3,4},{4,5},{5,6},{6,7},{8,9},{9,10},{10,11},{11... | collective-permute-start | bytes 27656 | tf_op jit(solution)/shard_map/ppermute | solution.py:23
  62.6 7.5 %collective-permute-start.4 = (f32[5,1,32,128]{3,0,2,1:T(8,128)S(1)}, f32[5,1,32,128]{3,0,2,1:T(8,128)S(1)}, u32[]{:S(2)}, u32[]{:S(2)}) collective-permute-start(f32[5,1,32,128]{3,0,2,1:T(8,128)S(1)} %get-tuple-element.57), channel_id=1, source_target_pairs={{8,0},{16,8},{24,16},{32,24},{40,32},{48,40},{56,48},{64,56},{72,6... | collective-permute-start | bytes 245768 | tf_op jit(solution)/shard_map/ppermute | solution.py:26
  64.6 7.5 %collective-permute-start.5 = (f32[5,1,32,128]{3,0,2,1:T(8,128)S(1)}, f32[5,1,32,128]{3,0,2,1:T(8,128)S(1)}, u32[]{:S(2)}, u32[]{:S(2)}) collective-permute-start(f32[5,1,32,128]{3,0,2,1:T(8,128)S(1)} %get-tuple-element.56), channel_id=1, source_target_pairs={{0,8},{8,16},{16,24},{24,32},{32,40},{40,48},{48,56},{56,64},{64,7... | collective-permute-start | bytes 245768 | tf_op jit(solution)/shard_map/ppermute | solution.py:23
  72.1 4.4 %collective-permute-start.6 = (f32[5,10,1,128]{3,0,2,1:T(8,128)S(1)}, f32[5,10,1,128]{3,0,2,1:T(8,128)S(1)}, u32[]{:S(2)}, u32[]{:S(2)}) collective-permute-start(f32[5,10,1,128]{3,0,2,1:T(8,128)S(1)} %get-tuple-element.47), channel_id=1, source_target_pairs={{1,0},{2,1},{3,2},{4,3},{5,4},{6,5},{7,6},{9,8},{10,9},{11,10},{12... | collective-permute-start | bytes 76808 | tf_op jit(solution)/shard_map/ppermute | solution.py:26
  73.4 4.0 %collective-permute-start.7 = (f32[5,10,1,128]{3,0,2,1:T(8,128)S(1)}, f32[5,10,1,128]{3,0,2,1:T(8,128)S(1)}, u32[]{:S(2)}, u32[]{:S(2)}) collective-permute-start(f32[5,10,1,128]{3,0,2,1:T(8,128)S(1)} %get-tuple-element.46), channel_id=1, source_target_pairs={{0,1},{1,2},{2,3},{3,4},{4,5},{5,6},{6,7},{8,9},{9,10},{10,11},{11... | collective-permute-start | bytes 76808 | tf_op jit(solution)/shard_map/ppermute | solution.py:23
  80.3 7.5 %collective-permute-start.8 = (f32[5,1,32,128]{3,0,2,1:T(8,128)S(1)}, f32[5,1,32,128]{3,0,2,1:T(8,128)S(1)}, u32[]{:S(2)}, u32[]{:S(2)}) collective-permute-start(f32[5,1,32,128]{3,0,2,1:T(8,128)S(1)} %get-tuple-element.55), channel_id=1, source_target_pairs={{8,0},{16,8},{24,16},{32,24},{40,32},{48,40},{56,48},{64,56},{72,6... | collective-permute-start | bytes 245768 | tf_op jit(solution)/shard_map/ppermute | solution.py:26
  82.2 7.4 %collective-permute-start.9 = (f32[5,1,32,128]{3,0,2,1:T(8,128)S(1)}, f32[5,1,32,128]{3,0,2,1:T(8,128)S(1)}, u32[]{:S(2)}, u32[]{:S(2)}) collective-permute-start(f32[5,1,32,128]{3,0,2,1:T(8,128)S(1)} %get-tuple-element.54), channel_id=1, source_target_pairs={{0,8},{8,16},{16,24},{24,32},{32,40},{40,48},{48,56},{56,64},{64,7... | collective-permute-start | bytes 245768 | tf_op jit(solution)/shard_map/ppermute | solution.py:23
  89.6 6.0 %collective-permute-start.10 = (f32[5,10,1,128]{3,0,2,1:T(8,128)S(1)}, f32[5,10,1,128]{3,0,2,1:T(8,128)S(1)}, u32[]{:S(2)}, u32[]{:S(2)}) collective-permute-start(f32[5,10,1,128]{3,0,2,1:T(8,128)S(1)} %get-tuple-element.45), channel_id=1, source_target_pairs={{1,0},{2,1},{3,2},{4,3},{5,4},{6,5},{7,6},{9,8},{10,9},{11,10},{12... | collective-permute-start | bytes 76808 | tf_op jit(solution)/shard_map/ppermute | solution.py:26
  90.9 10.4 %collective-permute-start.11 = (f32[5,10,1,128]{3,0,2,1:T(8,128)S(1)}, f32[5,10,1,128]{3,0,2,1:T(8,128)S(1)}, u32[]{:S(2)}, u32[]{:S(2)}) collective-permute-start(f32[5,10,1,128]{3,0,2,1:T(8,128)S(1)} %get-tuple-element.44), channel_id=1, source_target_pairs={{0,1},{1,2},{2,3},{3,4},{4,5},{5,6},{6,7},{8,9},{9,10},{10,11},{11... | collective-permute-start | bytes 76808 | tf_op jit(solution)/shard_map/ppermute | solution.py:23
  94.2 23.8 %collective-permute-start.22 = (f32[18,1,128]{2,1,0:T(1,128)S(1)}, f32[18,1,128]{2,1,0:T(1,128)S(1)}, u32[]{:S(2)}, u32[]{:S(2)}) collective-permute-start(f32[18,1,128]{2,1,0:T(1,128)S(1)} %get-tuple-element.73), channel_id=1, source_target_pairs={{1,0},{2,1},{3,2},{4,3},{5,4},{6,5},{7,6},{9,8},{10,9},{11,10},{12... | collective-permute-start | bytes 27656 | tf_op jit(solution)/shard_map/ppermute | solution.py:26
  95.5 22.5 %collective-permute-start.23 = (f32[18,1,128]{2,1,0:T(1,128)S(1)}, f32[18,1,128]{2,1,0:T(1,128)S(1)}, u32[]{:S(2)}, u32[]{:S(2)}) collective-permute-start(f32[18,1,128]{2,1,0:T(1,128)S(1)} %get-tuple-element.72), channel_id=1, source_target_pairs={{0,1},{1,2},{2,3},{3,4},{4,5},{5,6},{6,7},{8,9},{9,10},{10,11},{11... | collective-permute-start | bytes 27656 | tf_op jit(solution)/shard_map/ppermute | solution.py:23
  104.2 7.2 %collective-permute-start.12 = (f32[5,1,32,128]{3,0,2,1:T(8,128)S(1)}, f32[5,1,32,128]{3,0,2,1:T(8,128)S(1)}, u32[]{:S(2)}, u32[]{:S(2)}) collective-permute-start(f32[5,1,32,128]{3,0,2,1:T(8,128)S(1)} %get-tuple-element.53), channel_id=1, source_target_pairs={{8,0},{16,8},{24,16},{32,24},{40,32},{48,40},{56,48},{64,56},{72,6... | collective-permute-start | bytes 245768 | tf_op jit(solution)/shard_map/ppermute | solution.py:26
  106.1 7.5 %collective-permute-start.13 = (f32[5,1,32,128]{3,0,2,1:T(8,128)S(1)}, f32[5,1,32,128]{3,0,2,1:T(8,128)S(1)}, u32[]{:S(2)}, u32[]{:S(2)}) collective-permute-start(f32[5,1,32,128]{3,0,2,1:T(8,128)S(1)} %get-tuple-element.52), channel_id=1, source_target_pairs={{0,8},{8,16},{16,24},{24,32},{32,40},{40,48},{48,56},{56,64},{64,7... | collective-permute-start | bytes 245768 | tf_op jit(solution)/shard_map/ppermute | solution.py:23
  113.6 4.8 %collective-permute-start.14 = (f32[5,10,1,128]{3,0,2,1:T(8,128)S(1)}, f32[5,10,1,128]{3,0,2,1:T(8,128)S(1)}, u32[]{:S(2)}, u32[]{:S(2)}) collective-permute-start(f32[5,10,1,128]{3,0,2,1:T(8,128)S(1)} %get-tuple-element.43), channel_id=1, source_target_pairs={{1,0},{2,1},{3,2},{4,3},{5,4},{6,5},{7,6},{9,8},{10,9},{11,10},{12... | collective-permute-start | bytes 76808 | tf_op jit(solution)/shard_map/ppermute | solution.py:26
  114.9 3.9 %collective-permute-start.15 = (f32[5,10,1,128]{3,0,2,1:T(8,128)S(1)}, f32[5,10,1,128]{3,0,2,1:T(8,128)S(1)}, u32[]{:S(2)}, u32[]{:S(2)}) collective-permute-start(f32[5,10,1,128]{3,0,2,1:T(8,128)S(1)} %get-tuple-element.42), channel_id=1, source_target_pairs={{0,1},{1,2},{2,3},{3,4},{4,5},{5,6},{6,7},{8,9},{9,10},{10,11},{11... | collective-permute-start | bytes 76808 | tf_op jit(solution)/shard_map/ppermute | solution.py:23
  119.7 61.6 %copy-start.2 = (f32[16,32,128]{2,1,0:T(8,128)S(1)}, f32[16,32,128]{2,1,0:T(8,128)}, u32[]{:S(2)}) copy-start(f32[16,32,128]{2,1,0:T(8,128)} %param.23) | copy-start | bytes 786436
  182.7 5.9 %collective-permute-start.24 = (f32[1,32,128]{2,1,0:T(8,128)S(1)}, f32[1,32,128]{2,1,0:T(8,128)S(1)}, u32[]{:S(2)}, u32[]{:S(2)}) collective-permute-start(f32[1,32,128]{2,1,0:T(8,128)S(1)} %get-tuple-element.79), channel_id=1, source_target_pairs={{8,0},{16,8},{24,16},{32,24},{40,32},{48,40},{56,48},{64,56},{72,6... | collective-permute-start | bytes 49160 | tf_op jit(solution)/shard_map/ppermute | solution.py:26
  184.7 5.6 %collective-permute-start.25 = (f32[1,32,128]{2,1,0:T(8,128)S(1)}, f32[1,32,128]{2,1,0:T(8,128)S(1)}, u32[]{:S(2)}, u32[]{:S(2)}) collective-permute-start(f32[1,32,128]{2,1,0:T(8,128)S(1)} %get-tuple-element.78), channel_id=1, source_target_pairs={{0,8},{8,16},{16,24},{24,32},{32,40},{40,48},{48,56},{56,64},{64,7... | collective-permute-start | bytes 49160 | tf_op jit(solution)/shard_map/ppermute | solution.py:23
  190.3 4.3 %collective-permute-start.26 = (f32[18,1,128]{2,1,0:T(1,128)S(1)}, f32[18,1,128]{2,1,0:T(1,128)S(1)}, u32[]{:S(2)}, u32[]{:S(2)}) collective-permute-start(f32[18,1,128]{2,1,0:T(1,128)S(1)} %get-tuple-element.69), channel_id=1, source_target_pairs={{1,0},{2,1},{3,2},{4,3},{5,4},{6,5},{7,6},{9,8},{10,9},{11,10},{12... | collective-permute-start | bytes 27656 | tf_op jit(solution)/shard_map/ppermute | solution.py:26
  191.6 3.9 %collective-permute-start.27 = (f32[18,1,128]{2,1,0:T(1,128)S(1)}, f32[18,1,128]{2,1,0:T(1,128)S(1)}, u32[]{:S(2)}, u32[]{:S(2)}) collective-permute-start(f32[18,1,128]{2,1,0:T(1,128)S(1)} %get-tuple-element.68), channel_id=1, source_target_pairs={{0,1},{1,2},{2,3},{3,4},{4,5},{5,6},{6,7},{8,9},{9,10},{10,11},{11... | collective-permute-start | bytes 27656 | tf_op jit(solution)/shard_map/ppermute | solution.py:23
  196.2 5.9 %collective-permute-start.28 = (f32[1,32,128]{2,1,0:T(8,128)S(1)}, f32[1,32,128]{2,1,0:T(8,128)S(1)}, u32[]{:S(2)}, u32[]{:S(2)}) collective-permute-start(f32[1,32,128]{2,1,0:T(8,128)S(1)} %get-tuple-element.77), channel_id=1, source_target_pairs={{8,0},{16,8},{24,16},{32,24},{40,32},{48,40},{56,48},{64,56},{72,6... | collective-permute-start | bytes 49160 | tf_op jit(solution)/shard_map/ppermute | solution.py:26
  198.1 5.6 %collective-permute-start.29 = (f32[1,32,128]{2,1,0:T(8,128)S(1)}, f32[1,32,128]{2,1,0:T(8,128)S(1)}, u32[]{:S(2)}, u32[]{:S(2)}) collective-permute-start(f32[1,32,128]{2,1,0:T(8,128)S(1)} %get-tuple-element.76), channel_id=1, source_target_pairs={{0,8},{8,16},{16,24},{24,32},{32,40},{40,48},{48,56},{56,64},{64,7... | collective-permute-start | bytes 49160 | tf_op jit(solution)/shard_map/ppermute | solution.py:23
  203.8 6.4 %collective-permute-start.30 = (f32[18,1,128]{2,1,0:T(1,128)S(1)}, f32[18,1,128]{2,1,0:T(1,128)S(1)}, u32[]{:S(2)}, u32[]{:S(2)}) collective-permute-start(f32[18,1,128]{2,1,0:T(1,128)S(1)} %get-tuple-element.67), channel_id=1, source_target_pairs={{1,0},{2,1},{3,2},{4,3},{5,4},{6,5},{7,6},{9,8},{10,9},{11,10},{12... | collective-permute-start | bytes 27656 | tf_op jit(solution)/shard_map/ppermute | solution.py:26
  205.1 5.9 %collective-permute-start.31 = (f32[18,1,128]{2,1,0:T(1,128)S(1)}, f32[18,1,128]{2,1,0:T(1,128)S(1)}, u32[]{:S(2)}, u32[]{:S(2)}) collective-permute-start(f32[18,1,128]{2,1,0:T(1,128)S(1)} %get-tuple-element.66), channel_id=1, source_target_pairs={{0,1},{1,2},{2,3},{3,4},{4,5},{5,6},{6,7},{8,9},{9,10},{10,11},{11... | collective-permute-start | bytes 27656 | tf_op jit(solution)/shard_map/ppermute | solution.py:23
  211.8 6.2 %collective-permute-start.32 = (f32[1,32,128]{2,1,0:T(8,128)S(1)}, f32[1,32,128]{2,1,0:T(8,128)S(1)}, u32[]{:S(2)}, u32[]{:S(2)}) collective-permute-start(f32[1,32,128]{2,1,0:T(8,128)S(1)} %get-tuple-element.75), channel_id=1, source_target_pairs={{8,0},{16,8},{24,16},{32,24},{40,32},{48,40},{56,48},{64,56},{72,6... | collective-permute-start | bytes 49160 | tf_op jit(solution)/shard_map/ppermute | solution.py:26
  213.7 5.6 %collective-permute-start.33 = (f32[1,32,128]{2,1,0:T(8,128)S(1)}, f32[1,32,128]{2,1,0:T(8,128)S(1)}, u32[]{:S(2)}, u32[]{:S(2)}) collective-permute-start(f32[1,32,128]{2,1,0:T(8,128)S(1)} %get-tuple-element.74), channel_id=1, source_target_pairs={{0,8},{8,16},{16,24},{24,32},{32,40},{40,48},{48,56},{56,64},{64,7... | collective-permute-start | bytes 49160 | tf_op jit(solution)/shard_map/ppermute | solution.py:23
  219.4 6.3 %collective-permute-start.34 = (f32[18,1,128]{2,1,0:T(1,128)S(1)}, f32[18,1,128]{2,1,0:T(1,128)S(1)}, u32[]{:S(2)}, u32[]{:S(2)}) collective-permute-start(f32[18,1,128]{2,1,0:T(1,128)S(1)} %get-tuple-element.65), channel_id=1, source_target_pairs={{1,0},{2,1},{3,2},{4,3},{5,4},{6,5},{7,6},{9,8},{10,9},{11,10},{12... | collective-permute-start | bytes 27656 | tf_op jit(solution)/shard_map/ppermute | solution.py:26
  220.7 5.6 %collective-permute-start.35 = (f32[18,1,128]{2,1,0:T(1,128)S(1)}, f32[18,1,128]{2,1,0:T(1,128)S(1)}, u32[]{:S(2)}, u32[]{:S(2)}) collective-permute-start(f32[18,1,128]{2,1,0:T(1,128)S(1)} %get-tuple-element.64), channel_id=1, source_target_pairs={{0,1},{1,2},{2,3},{3,4},{4,5},{5,6},{6,7},{8,9},{9,10},{10,11},{11... | collective-permute-start | bytes 27656 | tf_op jit(solution)/shard_map/ppermute | solution.py:23
  226.6 102.4 %copy-start.13 = (f32[6]{0:T(128)S(1)}, f32[6]{0:T(128)}, u32[]{:S(2)}) copy-start(f32[6]{0:T(128)} %constant.130) | copy-start | bytes 76
  227.8 103.5 %copy-start.6 = (f32[16,32,128]{2,1,0:T(8,128)}, f32[16,32,128]{2,1,0:T(8,128)S(1)}, u32[]{:S(2)}) copy-start(f32[16,32,128]{2,1,0:T(8,128)S(1)} %divide_add_fusion) | copy-start | bytes 786436
  228.7 100.9 %all-to-all-start = ((f32[32,32,128]{2,1,0:T(8,128)}), f32[32,32,128]{2,1,0:T(8,128)S(1)}, u32[]{:S(2)}, u32[]{:S(2)}) async-start(f32[32,32,128]{2,1,0:T(8,128)} %stack.3), calls=%async_computation | async-start | bytes 1048576 | tf_op jit(solution)/shard_map/all_to_all | solution.py:14
  (3 other events, 27.3 us)
